TPU v7x, 128 devices: a whole 4x4x4 slice. The times are simulated.
128 devices in a mesh: ctx: 8 (over y, z_hi), tensor: 16 (over z_lo, x, core).
Axes of the slice: x: 4, y: 4, z: 4 (z_hi: 2, z_lo: 2; z = z_hi * 2 + z_lo), core: 2. Of those that a mesh axis runs over, the one named last changes fastest.
Arguments:
- tokens: bfloat16 [16384, 4096], P('ctx'), may hold values from -6 to 6
- norm_gain: float32 [4096], replicated, may hold values from 0.1 to 1.9
- w_in: bfloat16 [4096, 3, 4096], P(None, None, 'tensor'), may hold values from -0.09375 to 0.09375
- short_taps: float32 [3, 3, 4096], P(None, None, 'tensor'), may hold values from -3 to 3
- filter_taps: float32 [128, 4096], P(None, 'tensor'), may hold values from -0.2 to 0.2
- filter_decay: float32 [4096], P('tensor'), may hold values from 0.00234375 to 0.03125
- skip_gain: float32 [4096], P('tensor'), may hold values from -2 to 2
- w_out: bfloat16 [4096, 4096], P('tensor'), may hold values from -0.09375 to 0.09375
- slot_span: int32 [16], replicated, may hold values from 0 to 15, as said below
- span_reset: int32 [16], replicated, may hold values from 0 to 1, as said below
Outputs:
- block_out: bfloat16 [16384, 4096], P(('ctx', 'tensor'))
Inputs may be any that keep to these rules, and one draw needn't show every extreme that they name: slot_span is a permutation of 0 to 15; for each ctx index d its entries 2d and 2d + 1 name the spans in that index's rows, with slot_span[2d] < 8 and slot_span[2d + 1] = 15 - slot_span[2d]. `span_reset`: some span after the first has a reset and some has none.
All inputs are finite; a program needn't handle non-finite values.
Results may differ from a plain program's by a relative error of at most 0.022.
Values may be sent and summed in bfloat16 or wider, within the bound.
A program may use at most 192 MiB of HBM per device.

v0:
```python
import jax
import jax.numpy as jnp
from jax import lax
from jax.sharding import PartitionSpec as P

epsilon = 1e-06


def shards(
    tokens,
    norm_gain,
    w_in,
    short_taps,
    filter_taps,
    filter_decay,
    skip_gain,
    w_out,
    slot_span,
    span_reset,
):
    floats = tokens.astype(jnp.float32)
    normed = (
        floats
        * lax.rsqrt(jnp.mean(floats * floats, axis=1, keepdims=True) + epsilon)
        * norm_gain[None, :]
    ).astype(jnp.bfloat16)
    model_width = w_in.shape[0]
    channels = w_in.shape[2]
    weight = w_in.reshape(model_width, 3 * channels)
    projected = jnp.dot(normed, weight, preferred_element_type=jnp.float32).astype(jnp.bfloat16)
    row_count = projected.shape[0]
    span_len = row_count // 2
    tap_count = filter_taps.shape[0]
    tail_len = tap_count + 1
    by_span = projected.reshape(2, span_len, 3 * channels)
    tail_rows = by_span[:, span_len - tail_len :, :]
    ctx_count = lax.axis_size("ctx")
    span_total = 2 * ctx_count
    position = lax.axis_index("ctx")
    slot_ids = jnp.arange(span_total, dtype=jnp.int32)
    own_spans = lax.dynamic_slice_in_dim(slot_span, 2 * position, 2, 0)
    previous = own_spans - 1
    matches = slot_span[None, :] == previous[:, None]
    wanted = jnp.sum(jnp.where(matches, slot_ids[None, :], 0), axis=1)
    reset_own = jnp.sum(
        jnp.where(slot_ids[None, :] == own_spans[:, None], span_reset[None, :], 0), axis=1
    )
    use_tail = jnp.logical_and(own_spans > 0, reset_own == 0)
    shard_rows = lax.all_gather(tail_rows, "ctx", axis=0, tiled=True)
    local_ids = jnp.arange(shard_rows.shape[0], dtype=jnp.int32)
    chosen = (local_ids[None, :] == wanted[:, None]).astype(jnp.bfloat16)
    received = jnp.einsum("qk,krc->qrc", chosen, shard_rows, preferred_element_type=jnp.float32)
    tails_used = jnp.where(use_tail[:, None, None], received, 0.0)
    extended = jnp.concatenate([tails_used, by_span.astype(jnp.float32)], axis=1).reshape(
        2, tail_len + span_len, 3, channels
    )
    conv_len = tap_count - 1 + span_len
    smoothed = (
        short_taps[0] * extended[:, 2 : 2 + conv_len]
        + short_taps[1] * extended[:, 1 : 1 + conv_len]
        + short_taps[2] * extended[:, 0:conv_len]
    )
    gate_query = smoothed[:, tap_count - 1 :, 0]
    mixed_in = smoothed[:, :, 1] * smoothed[:, :, 2]
    lag_index = jnp.arange(tap_count, dtype=jnp.float32)
    response = filter_taps * jnp.exp(-filter_decay[None, :] * lag_index[:, None])

    def add_lags(tap_block, running):
        for within in range(8):
            offset = tap_block * 8 + within
            shifted = lax.dynamic_slice_in_dim(mixed_in, tap_count - 1 - offset, span_len, 1)
            running = (
                running + lax.dynamic_index_in_dim(response, offset, 0, keepdims=False) * shifted
            )
        return running

    filtered = lax.fori_loop(
        0, tap_count // 8, add_lags, jnp.zeros((2, span_len, channels), jnp.float32)
    )
    gated = (
        (gate_query * (filtered + skip_gain * mixed_in[:, tap_count - 1 :]))
        .astype(jnp.bfloat16)
        .reshape(row_count, channels)
    )
    out_rows = row_count // lax.axis_size("tensor")
    own_floats = lax.dynamic_slice_in_dim(floats, lax.axis_index("tensor") * out_rows, out_rows, 0)
    partial_all = jnp.dot(gated, w_out, preferred_element_type=jnp.float32)
    mixed = lax.psum_scatter(
        partial_all.astype(jnp.bfloat16), "tensor", scatter_dimension=0, tiled=True
    ).astype(jnp.float32)
    return (own_floats + mixed).astype(jnp.bfloat16)


def solution(mesh):
    in_specs = (
        P("ctx", None),
        P(),
        P(None, None, "tensor"),
        P(None, None, "tensor"),
        P(None, "tensor"),
        P("tensor"),
        P("tensor"),
        P("tensor", None),
        P(),
        P(),
    )
    out_specs = P(("ctx", "tensor"), None)
    return jax.shard_map(shards, mesh=mesh, in_specs=in_specs, out_specs=out_specs, check_vma=False)
```

profile of v0, /device:TPU:1, one launch (start us, length us, event | category | flops | bytes accessed | tf_op | source)
XLA Modules:
  0.0 439.9 jit_solution(16877619501126017305)
XLA Ops:
  6.5 0.0 copy-start
  6.5 0.0 all-gather.2.cloned.1.call-start
  6.5 7.3 %multiply_reduce_fusion = f32[2048]{0:T(1024)S(1)} fusion(bf16[2048,4096]{1,0:T(8,128)(2,1)} %param.12), kind=kLoop, calls=%fused_computation.17 | loop fusion | flops 25163776 | bytes 16785408 | tf_op jit(solution)/shard_map/reduce_sum | solution.py:24
  13.9 0.0 copy-start.9
  13.9 8.8 %copy.36 = bf16[4096,3,256]{0,2,1:T(8,128)(2,1)} copy(bf16[4096,3,256]{2,0,1:T(8,128)(2,1)} %param.14) | data formatting | bytes 12582912 | tf_op args[2]
  22.7 0.0 copy-done.9
  22.7 18.6 %fusion.13 = bf16[2048,768]{1,0:T(8,128)(2,1)S(1)} fusion(bf16[4096,768]{0,1:T(8,128)(2,1)} %bitcast.49, f32[4096]{0:T(1024)S(1)} %copy-done.9, f32[2048]{0:T(1024)S(1)} %add_rsqrt_fusion, bf16[2048,4096]{1,0:T(8,128)(2,1)} %param.12), kind=kOutput, calls=%fused_computation.29 | convolution fusion | flops 12920029184 | bytes 26238976 | tf_op jit(solution)/shard_map/dot_general | solution.py:30
  41.3 0.0 copy-start.2
  41.3 1.6 copy-done.2
  42.9 0.8 slice.44
  43.8 0.0 all-gather.2.cloned.1.call-update
  43.8 0.0 reduce-scatter.2.cloned.1.call-start
  43.9 0.0 copy-start.6
  43.9 0.0 copy-start.5
  43.9 0.0 copy-start.8
  43.9 0.0 copy-start.4
  43.9 0.0 copy-start.3
  43.9 5.1 %convert_element_type.28 = f32[2,1024,768]{2,1,0:T(8,128)} convert(bf16[2,1024,768]{2,1,0:T(8,128)(2,1)} %bitcast.52) | non-fusion elementwise | flops 1572864 | bytes 9437184 | tf_op jit(solution)/shard_map/convert_element_type | solution.py:54
  49.0 0.0 copy-done.6
  49.0 0.0 copy-done.5
  49.0 0.1 broadcast_add_fusion
  49.1 0.0 copy-done.8
  49.1 0.2 fusion.25
  49.3 0.0 copy-done.4
  49.4 0.0 copy-done.3
  49.4 61.4 %all-gather.2.cloned.1.call-done = bf16[16,129,768]{2,1,0:T(8,128)(2,1)} async-done(((bf16[2,129,768]{2,1,0:T(8,128)(2,1)}), bf16[16,129,768]{2,1,0:T(8,128)(2,1)}) %all-gather.2.cloned.1.call-update) | async-done | bytes 3170320 | tf_op jit(solution)/shard_map/all_gather | solution.py:49
  110.9 2.7 fusion.20
  113.6 0.1 copy.38
  113.7 6.2 %pad_maximum_fusion = f32[2,1153,768]{2,1,0:T(8,128)} fusion(f32[2,1024,768]{2,1,0:T(8,128)} %convert_element_type.28, f32[2,129,768]{2,1,0:T(8,128)S(1)} %copy.38), kind=kLoop, calls=%fused_computation.23 | loop fusion | flops 1771008 | bytes 14168064 | tf_op jit(solution)/shard_map/concatenate | solution.py:54
  119.9 8.4 %copy.39 = f32[2,1153,768]{1,2,0:T(8,128)} copy(f32[2,1153,768]{2,1,0:T(8,128)} %pad_maximum_fusion) | data formatting | bytes 14168064 | tf_op jit(solution)/shard_map/concatenate | solution.py:54
  128.2 9.7 %fusion.11 = f32[2,1151,3,256]{1,3,2,0:T(8,128)S(1)} fusion(f32[2,1153,3,256]{1,3,2,0:T(8,128)} %bitcast.48, f32[3,256]{1,0:T(4,128)S(1)} %get-tuple-element.207, f32[3,256]{1,0:T(4,128)S(1)} %get-tuple-element.208, f32[3,256]{1,0:T(4,128)S(1)} %get-tuple-element.206), kind=kLoop, calls=%fused_computation.25 | loop fusion | flops 8839680 | bytes 28296192 | tf_op jit(solution)/shard_map/add | solution.py:59
  137.9 0.0 copy-start.1
  137.9 2.9 copy-done.1
  140.9 1.7 fusion.16
  142.6 3.1 copy.41
  145.6 170.7 %while.17 = (s32[]{:T(128)}, f32[2,1024,256]{2,1,0:T(8,128)}, f32[128,256]{1,0:T(8,128)S(1)}, f32[2,1151,256]{2,1,0:T(8,128)}, s32[]{:T(128)}, /*index=5*/s32[]{...) while((s32[]{:T(128)}, f32[2,1024,256]{2,1,0:T(8,128)}, ...), condition=%wide.region_4.5_spmd.clone, body=%wide.region_3.4_spmd.clone.sunk | while | flops 8912963 | bytes 20997116 | solution.py:77
  145.6 10.2 %fusion.33 = f32[2,1024,256]{2,1,0:T(8,128)} fusion(f32[2,1024,256]{2,1,0:T(8,128)} %get-tuple-element.276, f32[2,1151,256]{2,1,0:T(8,128)} %get-tuple-element.301, s32[]{:T(128)S(6)} %select_n.238, s32[]{:T(128)S(6)} %select_n.239, s32[]{:T(128)S(6)} %select_n.240, s32[]{:T(128)S(6)} %select_n.241, s32[]{:T(128)S(6)} %select_n.242, ...), kind=kLoop, calls=%fused_computation.7.clone.1 | loop fusion | flops 8912896 | bytes 20979744 | tf_op jit(solution)/shard_map/while/body/eval_jaxpr/add | solution.py:73
  155.9 10.6 %fusion.33 = f32[2,1024,256]{2,1,0:T(8,128)} fusion(f32[2,1024,256]{2,1,0:T(8,128)} %get-tuple-element.276, f32[2,1151,256]{2,1,0:T(8,128)} %get-tuple-element.301, s32[]{:T(128)S(6)} %select_n.238, s32[]{:T(128)S(6)} %select_n.239, s32[]{:T(128)S(6)} %select_n.240, s32[]{:T(128)S(6)} %select_n.241, s32[]{:T(128)S(6)} %select_n.242, ...), kind=kLoop, calls=%fused_computation.7.clone.1 | loop fusion | flops 8912896 | bytes 20979744 | tf_op jit(solution)/shard_map/while/body/eval_jaxpr/add | solution.py:73
  166.6 10.8 %fusion.33 = f32[2,1024,256]{2,1,0:T(8,128)} fusion(f32[2,1024,256]{2,1,0:T(8,128)} %get-tuple-element.276, f32[2,1151,256]{2,1,0:T(8,128)} %get-tuple-element.301, s32[]{:T(128)S(6)} %select_n.238, s32[]{:T(128)S(6)} %select_n.239, s32[]{:T(128)S(6)} %select_n.240, s32[]{:T(128)S(6)} %select_n.241, s32[]{:T(128)S(6)} %select_n.242, ...), kind=kLoop, calls=%fused_computation.7.clone.1 | loop fusion | flops 8912896 | bytes 20979744 | tf_op jit(solution)/shard_map/while/body/eval_jaxpr/add | solution.py:73
  177.4 10.8 %fusion.33 = f32[2,1024,256]{2,1,0:T(8,128)} fusion(f32[2,1024,256]{2,1,0:T(8,128)} %get-tuple-element.276, f32[2,1151,256]{2,1,0:T(8,128)} %get-tuple-element.301, s32[]{:T(128)S(6)} %select_n.238, s32[]{:T(128)S(6)} %select_n.239, s32[]{:T(128)S(6)} %select_n.240, s32[]{:T(128)S(6)} %select_n.241, s32[]{:T(128)S(6)} %select_n.242, ...), kind=kLoop, calls=%fused_computation.7.clone.1 | loop fusion | flops 8912896 | bytes 20979744 | tf_op jit(solution)/shard_map/while/body/eval_jaxpr/add | solution.py:73
  188.2 10.8 %fusion.33 = f32[2,1024,256]{2,1,0:T(8,128)} fusion(f32[2,1024,256]{2,1,0:T(8,128)} %get-tuple-element.276, f32[2,1151,256]{2,1,0:T(8,128)} %get-tuple-element.301, s32[]{:T(128)S(6)} %select_n.238, s32[]{:T(128)S(6)} %select_n.239, s32[]{:T(128)S(6)} %select_n.240, s32[]{:T(128)S(6)} %select_n.241, s32[]{:T(128)S(6)} %select_n.242, ...), kind=kLoop, calls=%fused_computation.7.clone.1 | loop fusion | flops 8912896 | bytes 20979744 | tf_op jit(solution)/shard_map/while/body/eval_jaxpr/add | solution.py:73
  199.0 10.8 %fusion.33 = f32[2,1024,256]{2,1,0:T(8,128)} fusion(f32[2,1024,256]{2,1,0:T(8,128)} %get-tuple-element.276, f32[2,1151,256]{2,1,0:T(8,128)} %get-tuple-element.301, s32[]{:T(128)S(6)} %select_n.238, s32[]{:T(128)S(6)} %select_n.239, s32[]{:T(128)S(6)} %select_n.240, s32[]{:T(128)S(6)} %select_n.241, s32[]{:T(128)S(6)} %select_n.242, ...), kind=kLoop, calls=%fused_computation.7.clone.1 | loop fusion | flops 8912896 | bytes 20979744 | tf_op jit(solution)/shard_map/while/body/eval_jaxpr/add | solution.py:73
  209.8 10.8 %fusion.33 = f32[2,1024,256]{2,1,0:T(8,128)} fusion(f32[2,1024,256]{2,1,0:T(8,128)} %get-tuple-element.276, f32[2,1151,256]{2,1,0:T(8,128)} %get-tuple-element.301, s32[]{:T(128)S(6)} %select_n.238, s32[]{:T(128)S(6)} %select_n.239, s32[]{:T(128)S(6)} %select_n.240, s32[]{:T(128)S(6)} %select_n.241, s32[]{:T(128)S(6)} %select_n.242, ...), kind=kLoop, calls=%fused_computation.7.clone.1 | loop fusion | flops 8912896 | bytes 20979744 | tf_op jit(solution)/shard_map/while/body/eval_jaxpr/add | solution.py:73
  220.6 10.5 %fusion.33 = f32[2,1024,256]{2,1,0:T(8,128)} fusion(f32[2,1024,256]{2,1,0:T(8,128)} %get-tuple-element.276, f32[2,1151,256]{2,1,0:T(8,128)} %get-tuple-element.301, s32[]{:T(128)S(6)} %select_n.238, s32[]{:T(128)S(6)} %select_n.239, s32[]{:T(128)S(6)} %select_n.240, s32[]{:T(128)S(6)} %select_n.241, s32[]{:T(128)S(6)} %select_n.242, ...), kind=kLoop, calls=%fused_computation.7.clone.1 | loop fusion | flops 8912896 | bytes 20979744 | tf_op jit(solution)/shard_map/while/body/eval_jaxpr/add | solution.py:73
  231.1 10.6 %fusion.33 = f32[2,1024,256]{2,1,0:T(8,128)} fusion(f32[2,1024,256]{2,1,0:T(8,128)} %get-tuple-element.276, f32[2,1151,256]{2,1,0:T(8,128)} %get-tuple-element.301, s32[]{:T(128)S(6)} %select_n.238, s32[]{:T(128)S(6)} %select_n.239, s32[]{:T(128)S(6)} %select_n.240, s32[]{:T(128)S(6)} %select_n.241, s32[]{:T(128)S(6)} %select_n.242, ...), kind=kLoop, calls=%fused_computation.7.clone.1 | loop fusion | flops 8912896 | bytes 20979744 | tf_op jit(solution)/shard_map/while/body/eval_jaxpr/add | solution.py:73
  241.8 10.6 %fusion.33 = f32[2,1024,256]{2,1,0:T(8,128)} fusion(f32[2,1024,256]{2,1,0:T(8,128)} %get-tuple-element.276, f32[2,1151,256]{2,1,0:T(8,128)} %get-tuple-element.301, s32[]{:T(128)S(6)} %select_n.238, s32[]{:T(128)S(6)} %select_n.239, s32[]{:T(128)S(6)} %select_n.240, s32[]{:T(128)S(6)} %select_n.241, s32[]{:T(128)S(6)} %select_n.242, ...), kind=kLoop, calls=%fused_computation.7.clone.1 | loop fusion | flops 8912896 | bytes 20979744 | tf_op jit(solution)/shard_map/while/body/eval_jaxpr/add | solution.py:73
  252.4 10.6 %fusion.33 = f32[2,1024,256]{2,1,0:T(8,128)} fusion(f32[2,1024,256]{2,1,0:T(8,128)} %get-tuple-element.276, f32[2,1151,256]{2,1,0:T(8,128)} %get-tuple-element.301, s32[]{:T(128)S(6)} %select_n.238, s32[]{:T(128)S(6)} %select_n.239, s32[]{:T(128)S(6)} %select_n.240, s32[]{:T(128)S(6)} %select_n.241, s32[]{:T(128)S(6)} %select_n.242, ...), kind=kLoop, calls=%fused_computation.7.clone.1 | loop fusion | flops 8912896 | bytes 20979744 | tf_op jit(solution)/shard_map/while/body/eval_jaxpr/add | solution.py:73
  263.1 10.5 %fusion.33 = f32[2,1024,256]{2,1,0:T(8,128)} fusion(f32[2,1024,256]{2,1,0:T(8,128)} %get-tuple-element.276, f32[2,1151,256]{2,1,0:T(8,128)} %get-tuple-element.301, s32[]{:T(128)S(6)} %select_n.238, s32[]{:T(128)S(6)} %select_n.239, s32[]{:T(128)S(6)} %select_n.240, s32[]{:T(128)S(6)} %select_n.241, s32[]{:T(128)S(6)} %select_n.242, ...), kind=kLoop, calls=%fused_computation.7.clone.1 | loop fusion | flops 8912896 | bytes 20979744 | tf_op jit(solution)/shard_map/while/body/eval_jaxpr/add | solution.py:73
  273.6 10.7 %fusion.33 = f32[2,1024,256]{2,1,0:T(8,128)} fusion(f32[2,1024,256]{2,1,0:T(8,128)} %get-tuple-element.276, f32[2,1151,256]{2,1,0:T(8,128)} %get-tuple-element.301, s32[]{:T(128)S(6)} %select_n.238, s32[]{:T(128)S(6)} %select_n.239, s32[]{:T(128)S(6)} %select_n.240, s32[]{:T(128)S(6)} %select_n.241, s32[]{:T(128)S(6)} %select_n.242, ...), kind=kLoop, calls=%fused_computation.7.clone.1 | loop fusion | flops 8912896 | bytes 20979744 | tf_op jit(solution)/shard_map/while/body/eval_jaxpr/add | solution.py:73
  284.3 10.6 %fusion.33 = f32[2,1024,256]{2,1,0:T(8,128)} fusion(f32[2,1024,256]{2,1,0:T(8,128)} %get-tuple-element.276, f32[2,1151,256]{2,1,0:T(8,128)} %get-tuple-element.301, s32[]{:T(128)S(6)} %select_n.238, s32[]{:T(128)S(6)} %select_n.239, s32[]{:T(128)S(6)} %select_n.240, s32[]{:T(128)S(6)} %select_n.241, s32[]{:T(128)S(6)} %select_n.242, ...), kind=kLoop, calls=%fused_computation.7.clone.1 | loop fusion | flops 8912896 | bytes 20979744 | tf_op jit(solution)/shard_map/while/body/eval_jaxpr/add | solution.py:73
  295.0 10.8 %fusion.33 = f32[2,1024,256]{2,1,0:T(8,128)} fusion(f32[2,1024,256]{2,1,0:T(8,128)} %get-tuple-element.276, f32[2,1151,256]{2,1,0:T(8,128)} %get-tuple-element.301, s32[]{:T(128)S(6)} %select_n.238, s32[]{:T(128)S(6)} %select_n.239, s32[]{:T(128)S(6)} %select_n.240, s32[]{:T(128)S(6)} %select_n.241, s32[]{:T(128)S(6)} %select_n.242, ...), kind=kLoop, calls=%fused_computation.7.clone.1 | loop fusion | flops 8912896 | bytes 20979744 | tf_op jit(solution)/shard_map/while/body/eval_jaxpr/add | solution.py:73
  305.8 10.6 %fusion.33 = f32[2,1024,256]{2,1,0:T(8,128)} fusion(f32[2,1024,256]{2,1,0:T(8,128)} %get-tuple-element.276, f32[2,1151,256]{2,1,0:T(8,128)} %get-tuple-element.301, s32[]{:T(128)S(6)} %select_n.238, s32[]{:T(128)S(6)} %select_n.239, s32[]{:T(128)S(6)} %select_n.240, s32[]{:T(128)S(6)} %select_n.241, s32[]{:T(128)S(6)} %select_n.242, ...), kind=kLoop, calls=%fused_computation.7.clone.1 | loop fusion | flops 8912896 | bytes 20979744 | tf_op jit(solution)/shard_map/while/body/eval_jaxpr/add | solution.py:73
  316.4 0.0 copy-start.7
  316.4 2.9 copy.42
  319.3 0.0 copy-done.7
  319.3 5.2 %fusion.19 = bf16[2,1024,256]{1,2,0:T(8,128)(2,1)} fusion(f32[2,1024,256]{1,2,0:T(8,128)} %copy.42, f32[2,1151,256]{1,2,0:T(8,128)} %fusion.16, f32[2,1151,3,256]{1,3,2,0:T(8,128)} %copy-done.1, f32[256]{0:T(256)S(1)} %copy-done.7), kind=kLoop, calls=%fused_computation.37 | loop fusion | flops 2097152 | bytes 7341056 | tf_op jit(solution)/shard_map/convert_element_type | solution.py:82
  324.4 1.5 copy.43
  325.9 0.0 copy-done
  325.9 8.1 %convolution_convert_fusion = bf16[2048,4096]{1,0:T(8,128)(2,1)} fusion(bf16[2048,256]{1,0:T(8,128)(2,1)S(1)} %bitcast.50, bf16[256,4096]{1,0:T(8,128)(2,1)S(1)} %copy-done), kind=kOutput, calls=%fused_computation.22 | convolution fusion | flops 4303355904 | bytes 19922944 | tf_op jit(solution)/shard_map/dot_general | solution.py:87
  334.0 0.0 reduce-scatter.2.cloned.1.call-update
  334.0 18.8 %convert_element_type.25 = f32[2048,4096]{1,0:T(8,128)} convert(bf16[2048,4096]{1,0:T(8,128)(2,1)} %param.12) | non-fusion elementwise | flops 8388608 | bytes 50331648 | tf_op jit(solution)/shard_map/convert_element_type | solution.py:21
  352.8 77.2 %reduce-scatter.2.cloned.1.call-done = bf16[128,4096]{1,0:T(8,128)(2,1)} async-done(((bf16[2048,4096]{1,0:T(8,128)(2,1)}), bf16[128,4096]{1,0:T(8,128)(2,1)}) %reduce-scatter.2.cloned.1.call-update) | async-done | bytes 1048592 | tf_op jit(solution)/shard_map/reduce_scatter | solution.py:88
  430.0 3.1 add_convert_fusion
  (22 shorter events, 0.4 us)
Async XLA Ops:
  6.5 319.4 %copy-start = (bf16[256,4096]{1,0:T(8,128)(2,1)S(1)}, bf16[256,4096]{1,0:T(8,128)(2,1)}, u32[]{:S(2)}) copy-start(bf16[256,4096]{1,0:T(8,128)(2,1)} %param.19) | copy-start | bytes 6291460
  6.5 104.3 %all-gather.2.cloned.1.call-start = ((), (), s32[]{:S(2)}) async-start(), calls=%async_computation.1 | async-start | bytes 3760128 | tf_op jit(solution)/shard_map/all_gather | solution.py:49
  13.9 8.8 %copy-start.9 = (f32[4096]{0:T(1024)S(1)}, f32[4096]{0:T(1024)}, u32[]{:S(2)}) copy-start(f32[4096]{0:T(1024)} %param.13) | copy-start | bytes 49156
  41.3 1.7 copy-start.2
  43.8 386.2 %reduce-scatter.2.cloned.1.call-start = ((), (), s32[]{:S(2)}) async-start(), calls=%async_computation.2 | async-start | bytes 17825792 | tf_op jit(solution)/shard_map/reduce_scatter | solution.py:88
  43.9 5.1 %copy-start.6 = (f32[256]{0:T(256)S(1)}, f32[256]{0:T(256)}, u32[]{:S(2)}) copy-start(f32[256]{0:T(256)} %param.17) | copy-start | bytes 3076
  43.9 5.1 %copy-start.5 = (s32[16]{0:T(128)S(1)}, s32[16]{0:T(128)}, u32[]{:S(2)}) copy-start(s32[16]{0:T(128)} %param.20) | copy-start | bytes 196
  43.9 5.2 %copy-start.8 = (s32[16]{0:T(128)S(1)}, s32[16]{0:T(128)}, u32[]{:S(2)}) copy-start(s32[16]{0:T(128)} %param.21) | copy-start | bytes 196
  43.9 5.4 %copy-start.4 = (f32[3,3,256]{2,1,0:T(4,128)S(1)}, f32[3,3,256]{2,1,0:T(4,128)}, u32[]{:S(2)}) copy-start(f32[3,3,256]{2,1,0:T(4,128)} %param.15) | copy-start | bytes 27652
  43.9 5.4 %copy-start.3 = (f32[128,256]{1,0:T(8,128)S(1)}, f32[128,256]{1,0:T(8,128)}, u32[]{:S(2)}) copy-start(f32[128,256]{1,0:T(8,128)} %param.16) | copy-start | bytes 393220
  137.9 2.9 copy-start.1
  316.4 2.9 copy-start.7
Sparse Core Ops, SparseCore 0:
  43.9 66.8 all-gather.1
  334.1 95.7 reduce-scatter.1
where the time goes:
time: 441 us; the launch traced here: 440 us
  other arithmetic  228 us (52%)
  waiting for transfers between devices  139 us (32%)
  local copies, waits for them, and re-layouts  30.4 us (7%)
  matrix products  29.4 us (7%)
  between operations  13.6 us (3%)
    add x16, other arithmetic, add_lags(): running + lax.dynamic_index_in_dim(response, offset, 0, keepdims=False) *...  170 us
    reduce_scatter x1, waiting for transfers between devices, shards(): lax.psum_scatter(partial_all.astype(jnp.bfloat16), 'tensor', scatter_dime...  77.2 us
    all_gather x1, waiting for transfers between devices, shards(): shard_rows = lax.all_gather(tail_rows, 'ctx', axis=0, tiled=True)  61.4 us
    convert_element_type x1, other arithmetic, shards(): floats = tokens.astype(jnp.float32)  18.8 us
    dot_general x1, matrix products, shards(): jnp.dot(normed, weight, preferred_element_type=jnp.float32)  18.6 us
    unnamed x22, local copies, waits for them, and re-layouts  16.4 us
    add x1, other arithmetic, shards(): short_taps[0] * extended[:, 2:2 + conv_len]  9.69 us
  transfers between devices with their start and end apart: 2, of which 2 were waited for; matrix products, arithmetic and copies ran while one was open for 6% of the time, Pallas kernels for 0%

commit v1 on v0

v1 whole, which is shorter than its diff:
```python
import functools

import jax
import jax.numpy as jnp
import numpy as np
from jax import lax
from jax.experimental import pallas as pl
from jax.experimental.pallas import tpu as pltpu
from jax.sharding import PartitionSpec as P

epsilon = 1e-06
F32 = jnp.float32
BF16 = jnp.bfloat16
MESH = pl.DeviceIdType.MESH
HALO = 160


def split(value):
    high = value.astype(BF16)
    low = (value - high.astype(F32)).astype(BF16)
    return high, low


def transforms():
    points = 256
    k = np.arange(128)[:, None]
    n = np.arange(points)[None, :]
    forward = np.zeros((points, points))
    forward[:128] = np.cos(2 * np.pi * k * n / points)
    forward[128:] = np.sin(2 * np.pi * k * n / points)
    forward[128] = np.cos(np.pi * n[0])
    weight = np.full((points, 1), 2.0 / points)
    weight[0] = weight[128] = 1.0 / points
    inverse = (forward * weight)[:, 128:].T

    def halves(matrix):
        high = matrix.astype(jnp.bfloat16)
        low = (matrix - high.astype(np.float64)).astype(jnp.bfloat16)
        return np.stack([high, low])

    return halves(forward), halves(inverse)


def dot(a, b):
    return jnp.dot(a, b, preferred_element_type=F32)


def kernel(
    tokens,
    gain,
    w_in,
    short,
    taps,
    decay,
    skip,
    w_out,
    fwd,
    inv,
    slot_span,
    span_reset,
    out,
    tok,
    scaled,
    win,
    pr,
    spec,
    halo,
    gsend,
    grecv,
    wg,
    part,
    recv,
    own,
    tok_sem,
    win_sem,
    loc_sem,
    h_send,
    h_recv,
    g_send,
    g_recv,
    w_send,
    w_recv,
    r_send,
    r_recv,
):
    ctx = lax.axis_index("ctx")
    ten = lax.axis_index("tensor")
    z = ten // 8
    x = (ten // 2) % 4
    core = ten % 2
    oz = 1 - z
    oc = 1 - core
    octx = ctx + 1 - 2 * (ctx % 2)
    right = (x + 1) % 4
    left = (x + 3) % 4
    far = (x + 2) % 4

    def place(z_, x_, c_):
        return z_ * 8 + x_ * 2 + c_

    partner = (ctx, place(z, x, oc))
    zsame = (ctx, place(oz, x, core))
    zcross = (ctx, place(oz, x, oc))
    zother = (octx, place(oz, x, core))
    to_right = (ctx, place(z, right, core))
    to_left = (ctx, place(z, left, core))
    circle = [((ctx + d) % 8, ten) for d in range(1, 8)]
    peers = [partner, zsame, zcross, zother, to_right, to_left] + circle

    def block_of(i):
        j = i - 2
        s = jnp.where(i < 2, jnp.where(i == 0, oz, z), jnp.where(j < 3, oz, z))
        q = jnp.where(i < 2, 3, 2 - j % 3)
        return s, q

    def fetch(i):
        s, q = block_of(i)
        row = pl.multiple_of(s * 1024 + q * 256, 256)
        return pltpu.make_async_copy(
            tokens.at[pl.ds(row, 256)], tok.at[i % 2], tok_sem.at[i % 2]
        )

    barrier = pltpu.get_barrier_semaphore()
    for peer in peers:
        pl.semaphore_signal(barrier, inc=1, device_id=peer, device_id_type=MESH)
    fetch(jnp.int32(0)).start()
    win_copy = pltpu.make_async_copy(w_in, win, win_sem.at[0])
    win_copy.start()
    own_group = z * 2 + core
    own_rows = pl.multiple_of(own_group * 256, 256)
    wg_copy = pltpu.make_async_copy(w_out, wg.at[pl.ds(own_rows, 256)], loc_sem.at[0])
    wg_copy.start()
    tok_row = pl.multiple_of(ten * 128, 128)
    own_copy = pltpu.make_async_copy(tokens.at[pl.ds(tok_row, 128)], own, loc_sem.at[1])
    own_copy.start()
    pl.semaphore_wait(barrier, len(peers))

    pieces = [0, 2, 1, 3]

    def w_copy(index, source, rows, piece, peer):
        cols = pl.ds(piece * 1024, 1024)
        if source is None:
            src = wg.at[pl.ds(rows, 256), cols]
        else:
            src = source.at[:, cols]
        return pltpu.make_async_remote_copy(
            src_ref=src,
            dst_ref=wg.at[pl.ds(rows, 256), cols],
            send_sem=w_send.at[index],
            recv_sem=w_recv.at[index],
            device_id=peer,
            device_id_type=MESH,
        )

    z_rows = pl.multiple_of((oz * 2 + core) * 256, 256)
    w_partner = [w_copy(i, w_out, own_rows, p, partner) for i, p in enumerate(pieces)]
    w_z = [
        w_copy(4 + i, w_out, own_rows, p, zsame if p < 2 else zother)
        for i, p in enumerate(pieces)
    ]
    w_relay = [w_copy(8 + i, None, z_rows, p, partner) for i, p in enumerate(pieces)]
    for copy in w_z:
        copy.start()
    for copy in w_partner:
        copy.start()

    lag = lax.broadcasted_iota(jnp.int32, (128, 256), 0)
    response = taps[...] * jnp.exp(-decay[...] * lag.astype(F32))
    response = response + jnp.where(lag == 0, skip[...], 0.0)
    r_high, r_low = split(response)
    spectrum = (
        dot(fwd[0, :, :128], r_high) + dot(fwd[1, :, :128], r_high) + dot(fwd[0, :, :128], r_low)
    )
    cos_part = spectrum[:128]
    sin_part = spectrum[128:]
    spec[0] = cos_part
    spec[1] = jnp.where(lag == 0, 0.0, sin_part)
    spec[2] = jnp.where(lag == 0, sin_part, cos_part)

    def project(i):
        s, q = block_of(i)
        slot = i % 2
        fetch(i).wait()
        square = jnp.zeros((256, 128), F32)
        for chunk in range(8):
            cols = pl.ds(chunk * 512, 512)
            value = tok[slot, :, cols].astype(F32)
            scaled[:, cols] = (value * gain[:, cols]).astype(BF16)
            value = value * value
            for lane in range(4):
                square = square + value[:, lane * 128 : lane * 128 + 128]
        scale = lax.rsqrt(jnp.sum(square, axis=1, keepdims=True) * (1.0 / 4096) + epsilon)
        row = pl.multiple_of(8 + q * 256, 8)
        for p in range(3):
            pr[p, s, pl.ds(row, 256), :] = dot(scaled[...], win[p]) * scale

    def smooth(p, value, rows):
        return (
            short[0, pl.ds(p, 1), :] * value[8 : 8 + rows]
            + short[1, pl.ds(p, 1), :] * value[7 : 7 + rows]
            + short[2, pl.ds(p, 1), :] * value[6 : 6 + rows]
        )

    def tail_copies(s):
        index = ctx * 2 + s
        return [
            pltpu.make_async_remote_copy(
                src_ref=halo.at[index],
                dst_ref=halo.at[index],
                send_sem=h_send.at[d * 2 + s],
                recv_sem=h_recv.at[d * 2 + s],
                device_id=circle[d],
                device_id_type=MESH,
            )
            for d in range(7)
        ]

    def tail_step(i, carry):
        fetch(i + 1).start()
        project(i)
        s, _ = block_of(i)
        key = smooth(1, pr[1, s, pl.ds(896, 136), :], 128)
        val = smooth(2, pr[2, s, pl.ds(896, 136), :], 128)
        index = ctx * 2 + s
        halo[index, pl.ds(0, 128), :] = (key * val).astype(BF16)
        last = [pr[p, s, pl.ds(1024, 8), :] for p in range(3)]
        last.append(jnp.zeros((8, 256), F32))
        halo[index, pl.ds(128, 32), :] = jnp.concatenate(last, axis=0).astype(BF16)
        for copy in tail_copies(s):
            copy.start()
        return carry

    def convolve(mixed, query):
        high, low = split(mixed)
        outs = []
        for w in range(2):
            h = high[w * 128 : w * 128 + 256]
            l = low[w * 128 : w * 128 + 256]
            freq = dot(fwd[0], h) + dot(fwd[1], h) + dot(fwd[0], l)
            a = freq[:128]
            b = freq[128:]
            y = jnp.concatenate([a * spec[0] - b * spec[1], a * spec[1] + b * spec[2]], axis=0)
            y_high, y_low = split(y)
            outs.append(dot(inv[0], y_high) + dot(inv[1], y_high) + dot(inv[0], y_low))
        return (query * jnp.concatenate(outs, axis=0)).astype(BF16)

    own_cols = pl.ds(pl.multiple_of(own_group * 256, 256), 256)

    def gated_copy(index, send_row, peer, q):
        return pltpu.make_async_remote_copy(
            src_ref=gsend.at[pl.ds(send_row, 128)],
            dst_ref=grecv.at[pl.ds(pl.multiple_of(q * 128, 128), 128), own_cols],
            send_sem=g_send.at[index * 4 + q],
            recv_sem=g_recv.at[index * 4 + q],
            device_id=peer,
            device_id_type=MESH,
        )

    def gated_other(q):
        base = pl.multiple_of(q * 256, 256)
        same_row = pl.multiple_of(base + core * 128, 128)
        cross_row = pl.multiple_of(base + oc * 128, 128)
        return [gated_copy(0, same_row, zsame, q), gated_copy(1, cross_row, zcross, q)]

    def gated_mine(q):
        row = pl.multiple_of(1024 + q * 256 + oc * 128, 128)
        return [gated_copy(2, row, partner, q)]

    def emit(role, q, gated):
        row = pl.multiple_of(role * 1024 + q * 256, 256)
        gsend[pl.ds(row, 256), :] = gated
        if role == 0:
            copies = gated_other(q)
        else:
            keep = pl.multiple_of(row + core * 128, 128)
            grecv[pl.ds(pl.multiple_of(q * 128, 128), 128), own_cols] = gsend[pl.ds(keep, 128), :]
            copies = gated_mine(q)
        for copy in copies:
            copy.start()

    def main_step(role, last):
        def body(j, carry):
            i = 2 + role * 3 + j
            if last:

                @pl.when(j < 2)
                def _():
                    fetch(i + 1).start()
            else:
                fetch(i + 1).start()
            project(i)
            s = z if role else oz
            q = 3 - j
            wide = pl.ds(pl.multiple_of(q * 256 - 128, 128), 392)
            narrow = pl.ds(pl.multiple_of(q * 256, 256), 264)
            key = smooth(1, pr[1, s, wide, :], 384)
            val = smooth(2, pr[2, s, wide, :], 384)
            query = smooth(0, pr[0, s, narrow, :], 256)
            emit(role, q, convolve(key * val, query))
            return carry

        return body

    win_copy.wait()
    lax.fori_loop(0, 2, tail_step, 0)
    lax.fori_loop(0, 3, main_step(0, False), 0)
    lax.fori_loop(0, 3, main_step(1, True), 0)

    for s in range(2):
        for copy in tail_copies(s):
            copy.wait()
    for role in range(2):
        s = z if role else oz
        span = slot_span[2 * ctx + s]
        source = jnp.int32(0)
        for j in range(16):
            source = source + jnp.where(slot_span[j] == span - 1, j, 0)
        used = jnp.logical_and(span > 0, span_reset[span] == 0)
        mask = jnp.where(used, 1.0, 0.0)
        before = halo[source].astype(F32) * mask
        for p in range(3):
            pr[p, s, pl.ds(0, 8), :] = before[128 + p * 8 : 136 + p * 8]
        window = pl.ds(0, 264)
        key = smooth(1, pr[1, s, window, :], 256)
        val = smooth(2, pr[2, s, window, :], 256)
        query = smooth(0, pr[0, s, window, :], 256)
        mixed = jnp.concatenate([before[:128], key * val], axis=0)
        emit(role, jnp.int32(0), convolve(mixed, query))

    for i in range(4):
        w_z[i].wait()
        w_relay[i].start()
    wg_copy.wait()
    for q in range(4):
        for copy in gated_other(q) + gated_mine(q):
            copy.wait()

    def r_copy(index, block, piece, peer):
        cols = pl.ds(piece * 1024, 1024)
        return pltpu.make_async_remote_copy(
            src_ref=part.at[block, :, cols],
            dst_ref=recv.at[index],
            send_sem=r_send.at[index],
            recv_sem=r_recv.at[index],
            device_id=peer,
            device_id_type=MESH,
        )

    sums = []
    for half in range(2):
        a, b = half, 2 + half
        sums.append(
            [
                r_copy(6 * half + 0, far, a, to_right),
                r_copy(6 * half + 1, far, b, to_left),
                r_copy(6 * half + 2, right, b, to_right),
                r_copy(6 * half + 3, left, a, to_left),
                r_copy(6 * half + 4, right, a, to_right),
                r_copy(6 * half + 5, left, b, to_left),
            ]
        )
    for half in range(2):
        for i in (2 * half, 2 * half + 1):
            w_partner[i].wait()
            w_relay[i].wait()
            piece = pieces[i]

            def columns(j, carry, piece=piece):
                cols = pl.ds(pl.multiple_of(piece * 1024 + j * 256, 256), 256)
                value = dot(grecv[...], wg[:, cols]).astype(BF16)
                for q in range(4):
                    part[q, :, cols] = value[q * 128 : q * 128 + 128]
                return carry

            lax.fori_loop(0, 4, columns, 0)
        for copy in sums[half][:4]:
            copy.start()
    for half in range(2):
        for index, block, piece in ((0, right, half), (1, left, 2 + half)):
            sums[half][index].wait()
            cols = pl.ds(piece * 1024, 1024)
            part[block, :, cols] = (
                part[block, :, cols].astype(F32) + recv[6 * half + index].astype(F32)
            ).astype(BF16)
            sums[half][4 + index].start()
    own_copy.wait()
    for half in range(2):
        for piece, first, second in ((half, 3, 4), (2 + half, 2, 5)):
            sums[half][first].wait()
            sums[half][second].wait()
            cols = pl.ds(piece * 1024, 1024)
            total = part[x, :, cols].astype(F32) + recv[6 * half + first].astype(F32)
            total = total + recv[6 * half + second].astype(F32)
            out[:, cols] = (own[:, cols].astype(F32) + total).astype(BF16)


def shards(
    tokens,
    norm_gain,
    w_in,
    short_taps,
    filter_taps,
    filter_decay,
    skip_gain,
    w_out,
    slot_span,
    span_reset,
):
    fwd, inv = transforms()
    hbm = pl.BlockSpec(memory_space=pl.ANY)
    vmem = pl.BlockSpec(memory_space=pltpu.VMEM)
    smem = pl.BlockSpec(memory_space=pltpu.SMEM)
    return pl.pallas_call(
        kernel,
        out_shape=jax.ShapeDtypeStruct((128, 4096), BF16),
        in_specs=[hbm, vmem, hbm, vmem, vmem, vmem, vmem, hbm, vmem, vmem, smem, smem],
        out_specs=vmem,
        scratch_shapes=[
            pltpu.VMEM((2, 256, 4096), BF16),
            pltpu.VMEM((256, 4096), BF16),
            pltpu.VMEM((3, 4096, 256), BF16),
            pltpu.VMEM((3, 2, 1032, 256), F32),
            pltpu.VMEM((3, 128, 256), F32),
            pltpu.VMEM((16, HALO, 256), BF16),
            pltpu.VMEM((2048, 256), BF16),
            pltpu.VMEM((512, 1024), BF16),
            pltpu.VMEM((1024, 4096), BF16),
            pltpu.VMEM((4, 128, 4096), BF16),
            pltpu.VMEM((12, 128, 1024), BF16),
            pltpu.VMEM((128, 4096), BF16),
            pltpu.SemaphoreType.DMA((2,)),
            pltpu.SemaphoreType.DMA((1,)),
            pltpu.SemaphoreType.DMA((2,)),
            pltpu.SemaphoreType.DMA((14,)),
            pltpu.SemaphoreType.DMA((14,)),
            pltpu.SemaphoreType.DMA((12,)),
            pltpu.SemaphoreType.DMA((12,)),
            pltpu.SemaphoreType.DMA((12,)),
            pltpu.SemaphoreType.DMA((12,)),
            pltpu.SemaphoreType.DMA((12,)),
            pltpu.SemaphoreType.DMA((12,)),
        ],
        compiler_params=pltpu.CompilerParams(
            collective_id=0, has_side_effects=True, vmem_limit_bytes=60 * 1024 * 1024
        ),
    )(
        tokens,
        norm_gain.reshape(1, -1),
        jnp.transpose(w_in, (1, 0, 2)),
        short_taps,
        filter_taps,
        filter_decay.reshape(1, -1),
        skip_gain.reshape(1, -1),
        w_out,
        jnp.asarray(fwd),
        jnp.asarray(inv),
        slot_span,
        span_reset,
    )


def solution(mesh):
    in_specs = (
        P("ctx", None),
        P(),
        P(None, None, "tensor"),
        P(None, None, "tensor"),
        P(None, "tensor"),
        P("tensor"),
        P("tensor"),
        P("tensor", None),
        P(),
        P(),
    )
    out_specs = P(("ctx", "tensor"), None)
    return jax.shard_map(shards, mesh=mesh, in_specs=in_specs, out_specs=out_specs, check_vma=False)
```

time: 441 us -> 104 us (0.24)
  other arithmetic: 228 us -> 0 us
  waiting for transfers between devices: 139 us -> 0 us
  Pallas kernels: 0 us -> 101 us
  matrix products: 29.4 us -> 0 us
  local copies, waits for them, and re-layouts: 30.4 us -> 2.29 us
  between operations: 13.6 us -> 0.01 us
    add x17 -> x0, other arithmetic: 180 us -> none  [the longest x16 170 us: add_lags(): running + lax.dynamic_index_in_dim(response, offset, 0, keepdims=False) *...]
    pallas_call x0 -> x1, Pallas kernels: none -> 101 us  [shards(): pl.pallas_call(kernel, out_shape=jax.ShapeDtypeStruct((128, 4096), BF16),...]
    reduce_scatter x1 -> x0, waiting for transfers between devices: 77.2 us -> none  [shards(): lax.psum_scatter(partial_all.astype(jnp.bfloat16), 'tensor', scatter_dime...]
    all_gather x1 -> x0, waiting for transfers between devices: 61.4 us -> none  [shards(): shard_rows = lax.all_gather(tail_rows, 'ctx', axis=0, tiled=True)]
    convert_element_type x4 -> x0, other arithmetic: 32.1 us -> none  [the longest x1 18.8 us: shards(): floats = tokens.astype(jnp.float32)]
    dot_general x3 -> x0, matrix products: 29.4 us -> none  [the longest x1 18.6 us: shards(): jnp.dot(normed, weight, preferred_element_type=jnp.float32)]
    unnamed x22 -> x1, local copies, waits for them, and re-layouts: 16.4 us -> 2.29 us
    concatenate x1 -> x0, local copies, waits for them, and re-layouts: 8.35 us -> none  [shards(): jnp.concatenate([tails_used, by_span.astype(jnp.float32)], axis=1)]
  transfers between devices with their start and end apart: 2 -> 0, of which waited for: 2 -> 0; matrix products, arithmetic and copies ran while one was open for 6% -> 0% of each run, Pallas kernels for 0% -> 0%
where the time goes in v1:
time: 104 us; the launch traced here: 103 us
  Pallas kernels  101 us (97%)
  local copies, waits for them, and re-layouts  2.29 us (2%)
    pallas_call x1, Pallas kernels, shards(): pl.pallas_call(kernel, out_shape=jax.ShapeDtypeStruct((128, 4096), BF16),...  101 us
    unnamed x1, local copies, waits for them, and re-layouts  2.29 us

profile of v1, /device:TPU:1, one launch (start us, length us, event | category | flops | bytes accessed | tf_op | source)
XLA Modules:
  0.0 103.4 jit_solution(12004190453116781465)
XLA Ops:
  0.0 101.1 %shard_map.118 = bf16[128,4096]{1,0:T(8,128)(2,1)} custom-call(bf16[2048,4096]{1,0:T(8,128)(2,1)} %tokens.1, f32[1,4096]{1,0:T(1,128)} %bitcast.5, bf16[3,4096,256]{2,1,0:T(8,128)(2,1)} %bitcast.4, f32[3,3,256]{2,1,0:T(4,128)} %short.1, f32[128,256]{1,0:T(8,128)} %taps.1, f32[1,256]{1,0:T(1,128)} %bitcast.6, f32[1,256]{1,0:T(1,128)} %bitcast.7, ...), custom_call_target="tpu_custom_call" | custom-call | tf_op jit(solution)/shard_map/pallas_call | solution.py:413
  101.1 2.3 %copy.14 = bf16[128,4096]{1,0:T(8,128)(2,1)} copy(bf16[128,4096]{1,0:T(8,128)(2,1)} %shard_map.118) | data formatting | bytes 2097152

commit v2 on v1

v2 whole, which is shorter than its diff:
```python
import jax
import jax.numpy as jnp
import numpy as np
from jax import lax
from jax.experimental import pallas as pl
from jax.experimental.pallas import tpu as pltpu
from jax.sharding import PartitionSpec as P

epsilon = 1e-06
F32 = jnp.float32
BF16 = jnp.bfloat16
MESH = pl.DeviceIdType.MESH
HALO = 144


def split(value):
    high = value.astype(BF16)
    low = (value - high.astype(F32)).astype(BF16)
    return high, low


def transforms():
    points = 256
    k = np.arange(128)[:, None]
    n = np.arange(points)[None, :]
    forward = np.zeros((points, points))
    forward[:128] = np.cos(2 * np.pi * k * n / points)
    forward[128:] = np.sin(2 * np.pi * k * n / points)
    forward[128] = np.cos(np.pi * n[0])
    weight = np.full((points, 1), 2.0 / points)
    weight[0] = weight[128] = 1.0 / points
    inverse = (forward * weight)[:, 128:].T

    def halves(matrix):
        high = matrix.astype(jnp.bfloat16)
        low = (matrix - high.astype(np.float64)).astype(jnp.bfloat16)
        return np.stack([high, low])

    return halves(forward), halves(inverse)


def dot(a, b):
    return jnp.dot(a, b, preferred_element_type=F32)


def kernel(
    tokens,
    gain,
    w_in,
    short,
    taps,
    decay,
    skip,
    w_out,
    fwd,
    inv,
    slot_span,
    span_reset,
    out,
    tok,
    scaled,
    win,
    pr,
    spec,
    column,
    across,
    gsend,
    grecv,
    wg,
    part,
    recv,
    own,
    mix,
    gate,
    prods,
    tok_sem,
    win_sem,
    loc_sem,
    y_send,
    y_recv,
    z_send,
    z_recv,
    g_send,
    g_recv,
    w_send,
    w_recv,
    r_send,
    r_recv,
):
    ctx = lax.axis_index("ctx")
    ten = lax.axis_index("tensor")
    y = ctx // 2
    zh = ctx % 2
    z = ten // 8
    x = (ten // 2) % 4
    core = ten % 2
    oz = 1 - z
    oc = 1 - core
    octx = y * 2 + 1 - zh
    right = (x + 1) % 4
    left = (x + 3) % 4
    far = (x + 2) % 4

    def place(z_, x_, c_):
        return z_ * 8 + x_ * 2 + c_

    partner = (ctx, place(z, x, oc))
    zsame = (ctx, place(oz, x, core))
    zcross = (ctx, place(oz, x, oc))
    zother = (octx, place(oz, x, core))
    zfar = (octx, ten)
    to_right = (ctx, place(z, right, core))
    to_left = (ctx, place(z, left, core))
    y_peers = [(((y + d) % 4) * 2 + zh, ten) for d in (2, 1, 3)]
    peers = [partner, zsame, zcross, zother, zfar, to_right, to_left] + y_peers

    first = [(oz, 880, 144), (z, 880, 144)]
    second = [(oz, 768, 112), (z, 768, 112)]

    def block_of(i):
        j = i - 2
        return jnp.where(j < 3, oz, z), 2 - j % 3

    def pieces_of(i):
        if isinstance(i, int) and i < 2:
            return (first, second)[i]
        s, q = block_of(i)
        return [(s, q * 256, 256)]

    def fetch(i):
        offset = 0
        copies = []
        for s, start, count in pieces_of(i):
            row = pl.multiple_of(s * 1024 + start, 16)
            index = (i % 2) * 2 + len(copies)
            copies.append(
                pltpu.make_async_copy(
                    tokens.at[pl.ds(row, count)],
                    tok.at[i % 2, pl.ds(offset, count)],
                    tok_sem.at[index],
                )
            )
            offset += count
        return copies

    def start(copies):
        for copy in copies:
            copy.start()

    def wait(copies):
        for copy in copies:
            copy.wait()

    barrier = pltpu.get_barrier_semaphore()
    for peer in peers:
        pl.semaphore_signal(barrier, inc=1, device_id=peer, device_id_type=MESH)
    own_group = z * 2 + core
    own_rows = pl.multiple_of(own_group * 256, 256)
    wg_copy = pltpu.make_async_copy(w_out, wg.at[pl.ds(own_rows, 256)], loc_sem.at[0])
    wg_copy.start()
    start(fetch(0))
    win_copies = [pltpu.make_async_copy(w_in.at[p], win.at[p], win_sem.at[p]) for p in range(3)]
    start(win_copies)
    start(fetch(1))
    tok_row = pl.multiple_of(ten * 128, 128)
    own_copy = pltpu.make_async_copy(tokens.at[pl.ds(tok_row, 128)], own, loc_sem.at[1])
    own_copy.start()
    wg_copy.wait()
    pl.semaphore_wait(barrier, len(peers))

    def w_copy(index, rows, chunk, peer):
        cols = pl.ds(chunk * 512, 512)
        return pltpu.make_async_remote_copy(
            src_ref=wg.at[pl.ds(rows, 256), cols],
            dst_ref=wg.at[pl.ds(rows, 256), cols],
            send_sem=w_send.at[index],
            recv_sem=w_recv.at[index],
            device_id=peer,
            device_id_type=MESH,
        )

    z_rows = pl.multiple_of((oz * 2 + core) * 256, 256)
    direct = (0, 1, 7)
    w_partner = [w_copy(c, own_rows, c, partner) for c in range(8)]
    w_z = [w_copy(8 + c, own_rows, c, zsame if c in direct else zother) for c in range(8)]
    w_relay = [w_copy(16 + c, z_rows, c, partner) for c in range(8)]

    def relay(chunks):
        for c in chunks:
            w_z[c].wait_recv()
            w_relay[c].start()

    start([w_z[0], w_z[4], w_z[1], w_z[5], w_z[2]])
    start([w_partner[c] for c in (0, 4, 1, 5, 2, 6, 3, 7)])

    lag = lax.broadcasted_iota(jnp.int32, (128, 256), 0)
    response = taps[...] * jnp.exp(-decay[...] * lag.astype(F32))
    response = response + jnp.where(lag == 0, skip[...], 0.0)
    r_high, r_low = split(response)
    spectrum = (
        dot(fwd[0, :, :128], r_high) + dot(fwd[1, :, :128], r_high) + dot(fwd[0, :, :128], r_low)
    )
    cos_part = spectrum[:128]
    sin_part = spectrum[128:]
    spec[0] = cos_part
    spec[1] = jnp.where(lag == 0, 0.0, sin_part)
    spec[2] = jnp.where(lag == 0, sin_part, cos_part)

    def prepare(i):
        slot = i % 2
        rows = sum(count for _, _, count in pieces_of(i))
        square = jnp.zeros((rows, 128), F32)
        for chunk in range(8):
            cols = pl.ds(chunk * 512, 512)
            value = tok[slot, pl.ds(0, rows), cols].astype(F32)
            scaled[pl.ds(0, rows), cols] = (value * gain[:, cols]).astype(BF16)
            value = value * value
            for lane in range(4):
                square = square + value[:, lane * 128 : lane * 128 + 128]
        return lax.rsqrt(jnp.sum(square, axis=1, keepdims=True) * (1.0 / 4096) + epsilon)

    def project_part(i, p, scale):
        layout = pieces_of(i)
        rows = sum(count for _, _, count in layout)
        value = dot(scaled[pl.ds(0, rows), :], win[p]) * scale
        offset = 0
        for s, begin, count in layout:
            row = pl.multiple_of(8 + begin, 8)
            pr[p, s, pl.ds(row, count), :] = value[offset : offset + count]
            offset += count

    def project(i):
        scale = prepare(i)
        for p in range(3):
            project_part(i, p, scale)

    def smooth(p, value, rows):
        return (
            short[0, pl.ds(p, 1), :] * value[8 : 8 + rows]
            + short[1, pl.ds(p, 1), :] * value[7 : 7 + rows]
            + short[2, pl.ds(p, 1), :] * value[6 : 6 + rows]
        )

    def y_copies(s):
        index = y * 2 + s
        return [
            pltpu.make_async_remote_copy(
                src_ref=column.at[index],
                dst_ref=column.at[index],
                send_sem=y_send.at[d * 2 + s],
                recv_sem=y_recv.at[d * 2 + s],
                device_id=y_peers[d],
                device_id_type=MESH,
            )
            for d in range(3)
        ]

    line = lax.broadcasted_iota(jnp.int32, (8, 256), 0)

    def send_tail(s):
        index = y * 2 + s
        key = smooth(1, pr[1, s, pl.ds(896, 136), :], 128)
        val = smooth(2, pr[2, s, pl.ds(896, 136), :], 128)
        column[index, pl.ds(0, 128), :] = (key * val).astype(BF16)
        last = [pr[p, s, pl.ds(1024, 8), :] for p in range(3)]
        pair = jnp.where(line >= 6, last[0], pltpu.roll(last[1], 6, 0))
        column[index, pl.ds(128, 16), :] = jnp.concatenate([pair, last[2]], axis=0).astype(BF16)
        start(y_copies(s))

    def wanted(holder, s):
        span = slot_span[2 * holder + s]
        index = jnp.int32(0)
        half = jnp.int32(0)
        for j in range(16):
            hit = slot_span[j] == span - 1
            index = index + jnp.where(hit, (j // 4) * 2 + j % 2, 0)
            half = half + jnp.where(hit, (j // 2) % 2, 0)
        used = jnp.logical_and(span > 0, span_reset[span] == 0)
        return index, half, used

    z_copy = pltpu.make_async_remote_copy(
        src_ref=across.at[0],
        dst_ref=across.at[1],
        send_sem=z_send.at[0],
        recv_sem=z_recv.at[0],
        device_id=zfar,
        device_id_type=MESH,
    )

    def send_across():
        for s in range(2):
            for copy in y_copies(s):
                copy.wait_recv()
        for s in range(2):
            index, _, _ = wanted(octx, s)
            across[0, s] = column[index]
        z_copy.start()

    def to_spectrum(window):
        freq = dot(fwd[0], window)
        a = freq[:128]
        b = freq[128:]
        prod = jnp.concatenate([a * spec[0] - b * spec[1], a * spec[1] + b * spec[2]], axis=0)
        return prod.astype(BF16)

    def convolve(mixed, query):
        mixed = mixed.astype(BF16)
        outs = [dot(inv[0], to_spectrum(mixed[w * 128 : w * 128 + 256])) for w in range(2)]
        return (query * jnp.concatenate(outs, axis=0)).astype(BF16)

    own_cols = pl.ds(pl.multiple_of(own_group * 256, 256), 256)

    def gated_copy(index, send_row, peer, q):
        return pltpu.make_async_remote_copy(
            src_ref=gsend.at[pl.ds(send_row, 128)],
            dst_ref=grecv.at[pl.ds(pl.multiple_of(q * 128, 128), 128), own_cols],
            send_sem=g_send.at[index * 4 + q],
            recv_sem=g_recv.at[index * 4 + q],
            device_id=peer,
            device_id_type=MESH,
        )

    def gated_other(q):
        base = pl.multiple_of(q * 256, 256)
        same_row = pl.multiple_of(base + core * 128, 128)
        cross_row = pl.multiple_of(base + oc * 128, 128)
        return [gated_copy(0, same_row, zsame, q), gated_copy(1, cross_row, zcross, q)]

    def gated_mine(q):
        row = pl.multiple_of(1024 + q * 256 + oc * 128, 128)
        return [gated_copy(2, row, partner, q)]

    def keep(q):
        row = pl.multiple_of(1024 + q * 256 + core * 128, 128)
        grecv[pl.ds(pl.multiple_of(q * 128, 128), 128), own_cols] = gsend[pl.ds(row, 128), :]

    def smooth_block(role, q):
        s = jnp.where(role == 0, oz, z)
        wide = pl.ds(pl.multiple_of(q * 256 - 128, 128), 392)
        narrow = pl.ds(pl.multiple_of(q * 256, 256), 264)
        key = smooth(1, pr[1, s, wide, :], 384)
        val = smooth(2, pr[2, s, wide, :], 384)
        return key * val, smooth(0, pr[0, s, narrow, :], 256)

    def filter_block(role, q):
        row = pl.multiple_of(role * 1024 + q * 256, 256)
        gsend[pl.ds(row, 256), :] = convolve(*smooth_block(role, q))

    def filter_and_project(role, q, i):
        row = role * 1024 + q * 256
        mixed, query = smooth_block(role, q)
        mix[...] = mixed.astype(BF16)
        gate[...] = query
        scale = prepare(i)
        project_part(i, 0, scale)
        for w in range(2):
            prods[w] = to_spectrum(mix[pl.ds(w * 128, 256), :])
        project_part(i, 1, scale)
        for w in range(2):
            half = pl.ds(pl.multiple_of(row + w * 128, 128), 128)
            gsend[half, :] = (gate[pl.ds(w * 128, 128), :] * dot(inv[0], prods[w])).astype(BF16)
        project_part(i, 2, scale)

    def filter_first(role):
        s = oz if role == 0 else z
        index, half, used = wanted(ctx, s)
        mask_here = jnp.where(jnp.logical_and(used, half == zh), 1.0, 0.0)
        mask_across = jnp.where(jnp.logical_and(used, half != zh), 1.0, 0.0)
        before = column[index].astype(F32) * mask_here + across[1, s].astype(F32) * mask_across
        pair = before[128:136]
        pr[0, s, pl.ds(0, 8), :] = pair
        pr[1, s, pl.ds(0, 8), :] = pltpu.roll(pair, 2, 0)
        pr[2, s, pl.ds(0, 8), :] = before[136:144]
        window = pl.ds(0, 264)
        key = smooth(1, pr[1, s, window, :], 256)
        val = smooth(2, pr[2, s, window, :], 256)
        query = smooth(0, pr[0, s, window, :], 256)
        mixed = jnp.concatenate([before[:128], key * val], axis=0)
        gsend[pl.ds(role * 1024, 256), :] = convolve(mixed, query)

    wait(fetch(0))
    scale = prepare(0)
    start(fetch(2))
    for p in range(3):
        win_copies[p].wait()
        project_part(0, p, scale)
    for s in range(2):
        send_tail(s)
    wait(fetch(1))
    project(1)
    start(fetch(3))
    wait(fetch(2))
    project(2)

    def main_step(i, carry):
        j = i - 3
        role = jnp.where(j < 3, 0, 1)
        q = 3 - j % 3

        @pl.when(i < 7)
        def _():
            start(fetch(i + 1))

        wait(fetch(i))
        filter_and_project(role, q, i)

        @pl.when(j < 3)
        def _():
            start(gated_other(q))

        @pl.when(j >= 3)
        def _():
            keep(q)
            start(gated_mine(q))

        @pl.when(j == 0)
        def _():
            relay((0, 4))

        @pl.when(j == 1)
        def _():
            relay((1, 5))
            w_z[6].start()

        @pl.when(j == 2)
        def _():
            send_across()
            start([w_z[3], w_z[7]])

        @pl.when(j == 3)
        def _():
            relay((2,))

        return carry

    lax.fori_loop(3, 8, main_step, 0)
    filter_block(1, jnp.int32(1))
    keep(1)
    start(gated_mine(1))

    def r_copy(index, block, chunk, peer):
        cols = pl.ds(chunk * 512, 512)
        return pltpu.make_async_remote_copy(
            src_ref=part.at[block, :, cols],
            dst_ref=recv.at[index],
            send_sem=r_send.at[index],
            recv_sem=r_recv.at[index],
            device_id=peer,
            device_id_type=MESH,
        )

    sums = []
    for r in range(4):
        a, b = r, 4 + r
        sums.append(
            [
                (far, r_copy(6 * r + 0, far, a, to_right)),
                (far, r_copy(6 * r + 1, far, b, to_left)),
                (right, r_copy(6 * r + 2, right, b, to_right)),
                (left, r_copy(6 * r + 3, left, a, to_left)),
                (right, r_copy(6 * r + 4, right, a, to_right)),
                (left, r_copy(6 * r + 5, left, b, to_left)),
            ]
        )

    def multiply(r, begin, blocks):
        def columns(k, carry):
            cols = pl.ds(pl.multiple_of((k // 2) * 2048 + r * 512 + (k % 2) * 256, 256), 256)
            value = dot(grecv[pl.ds(begin * 128, blocks * 128), :], wg[:, cols]).astype(BF16)
            for q in range(blocks):
                part[begin + q, :, cols] = value[q * 128 : q * 128 + 128]
            return carry

        lax.fori_loop(0, 4, columns, 0)

    def send_own(r, ready):
        for block, copy in sums[r][:4]:
            if ready is None:
                copy.start()
            else:

                @pl.when(ready(block))
                def _(copy=copy):
                    copy.start()

    def add_and_send(r, index):
        block, copy = sums[r][4 + index]
        sums[r][index][1].wait_recv()
        cols = pl.ds((r + 4 * index) * 512, 512)
        part[block, :, cols] = (
            part[block, :, cols].astype(F32) + recv[6 * r + index].astype(F32)
        ).astype(BF16)
        copy.start()

    def pass_on(r, ready):
        for index in range(2):
            if ready is None:
                add_and_send(r, index)
            else:

                @pl.when(ready(sums[r][4 + index][0]))
                def _(index=index):
                    add_and_send(r, index)

    def w_ready(r):
        for c in (r, 4 + r):
            w_partner[c].wait_recv()
            w_relay[c].wait_recv()

    early = lambda block: block != 0
    late = lambda block: block == 0

    def gated_ready(q):
        for copy in gated_other(q) + gated_mine(q):
            copy.wait_recv()

    for q in (3, 2, 1):
        gated_ready(q)
    for r in range(2):
        w_ready(r)
        multiply(r, 1, 3)
        send_own(r, early)

    z_copy.wait_recv()
    filter_first(0)
    start(gated_other(0))
    filter_first(1)
    keep(0)
    start(gated_mine(0))
    relay((6,))
    gated_ready(0)
    for r in range(2):
        multiply(r, 0, 1)
        send_own(r, late)
    w_ready(2)
    multiply(2, 0, 4)
    send_own(2, None)
    relay((3, 7))
    for r in range(2):
        pass_on(r, early)
    w_ready(3)
    multiply(3, 0, 4)
    send_own(3, None)
    for r in range(2):
        pass_on(r, late)
    for r in (2, 3):
        pass_on(r, None)
    own_copy.wait()
    for r in range(4):
        for chunk, near, passed in ((r, 3, 4), (4 + r, 2, 5)):
            sums[r][near][1].wait_recv()
            sums[r][passed][1].wait_recv()
            cols = pl.ds(chunk * 512, 512)
            total = part[x, :, cols].astype(F32) + recv[6 * r + near].astype(F32)
            total = total + recv[6 * r + passed].astype(F32)
            out[:, cols] = (own[:, cols].astype(F32) + total).astype(BF16)

    for s in range(2):
        for copy in y_copies(s):
            copy.wait_send()
    z_copy.wait_send()
    for copy in w_partner + w_z + w_relay:
        copy.wait_send()
    for q in range(4):
        for copy in gated_other(q) + gated_mine(q):
            copy.wait_send()
    for r in range(4):
        for _, copy in sums[r]:
            copy.wait_send()


def shards(
    tokens,
    norm_gain,
    w_in,
    short_taps,
    filter_taps,
    filter_decay,
    skip_gain,
    w_out,
    slot_span,
    span_reset,
):
    fwd, inv = transforms()
    hbm = pl.BlockSpec(memory_space=pl.ANY)
    vmem = pl.BlockSpec(memory_space=pltpu.VMEM)
    smem = pl.BlockSpec(memory_space=pltpu.SMEM)
    return pl.pallas_call(
        kernel,
        out_shape=jax.ShapeDtypeStruct((128, 4096), BF16),
        in_specs=[hbm, vmem, hbm, vmem, vmem, vmem, vmem, hbm, vmem, vmem, smem, smem],
        out_specs=vmem,
        scratch_shapes=[
            pltpu.VMEM((2, 288, 4096), BF16),
            pltpu.VMEM((288, 4096), BF16),
            pltpu.VMEM((3, 4096, 256), BF16),
            pltpu.VMEM((3, 2, 1032, 256), F32),
            pltpu.VMEM((3, 128, 256), F32),
            pltpu.VMEM((8, HALO, 256), BF16),
            pltpu.VMEM((2, 2, HALO, 256), BF16),
            pltpu.VMEM((2048, 256), BF16),
            pltpu.VMEM((512, 1024), BF16),
            pltpu.VMEM((1024, 4096), BF16),
            pltpu.VMEM((4, 128, 4096), BF16),
            pltpu.VMEM((24, 128, 512), BF16),
            pltpu.VMEM((128, 4096), BF16),
            pltpu.VMEM((384, 256), BF16),
            pltpu.VMEM((256, 256), F32),
            pltpu.VMEM((2, 256, 256), BF16),
            pltpu.SemaphoreType.DMA((4,)),
            pltpu.SemaphoreType.DMA((3,)),
            pltpu.SemaphoreType.DMA((2,)),
            pltpu.SemaphoreType.DMA((6,)),
            pltpu.SemaphoreType.DMA((6,)),
            pltpu.SemaphoreType.DMA((1,)),
            pltpu.SemaphoreType.DMA((1,)),
            pltpu.SemaphoreType.DMA((12,)),
            pltpu.SemaphoreType.DMA((12,)),
            pltpu.SemaphoreType.DMA((24,)),
            pltpu.SemaphoreType.DMA((24,)),
            pltpu.SemaphoreType.DMA((24,)),
            pltpu.SemaphoreType.DMA((24,)),
        ],
        compiler_params=pltpu.CompilerParams(
            collective_id=0, has_side_effects=True, vmem_limit_bytes=60 * 1024 * 1024
        ),
    )(
        tokens,
        norm_gain.reshape(1, -1),
        jnp.transpose(w_in, (1, 0, 2)),
        short_taps,
        filter_taps,
        filter_decay.reshape(1, -1),
        skip_gain.reshape(1, -1),
        w_out,
        jnp.asarray(fwd),
        jnp.asarray(inv),
        slot_span,
        span_reset,
    )


def solution(mesh):
    in_specs = (
        P("ctx", None),
        P(),
        P(None, None, "tensor"),
        P(None, None, "tensor"),
        P(None, "tensor"),
        P("tensor"),
        P("tensor"),
        P("tensor", None),
        P(),
        P(),
    )
    out_specs = P(("ctx", "tensor"), None)
    return jax.shard_map(shards, mesh=mesh, in_specs=in_specs, out_specs=out_specs, check_vma=False)
```

time: 104 us -> 78.7 us (0.76)
  Pallas kernels: 101 us -> 76.2 us
    pallas_call x1, Pallas kernels: 101 us -> 76.2 us  [shards(): pl.pallas_call(kernel, out_shape=jax.ShapeDtypeStruct((128, 4096), BF16),...]
where the time goes in v2:
time: 78.7 us; the launch traced here: 78.5 us
  Pallas kernels  76.2 us (97%)
  local copies, waits for them, and re-layouts  2.29 us (3%)
    pallas_call x1, Pallas kernels, shards(): pl.pallas_call(kernel, out_shape=jax.ShapeDtypeStruct((128, 4096), BF16),...  76.2 us
    unnamed x1, local copies, waits for them, and re-layouts  2.29 us

profile of v2, /device:TPU:1, one launch (start us, length us, event | category | flops | bytes accessed | tf_op | source)
XLA Modules:
  0.0 78.5 jit_solution(8106965233769449441)
XLA Ops:
  0.0 76.2 %shard_map.118 = bf16[128,4096]{1,0:T(8,128)(2,1)} custom-call(bf16[2048,4096]{1,0:T(8,128)(2,1)} %tokens.1, f32[1,4096]{1,0:T(1,128)} %bitcast.5, bf16[3,4096,256]{2,1,0:T(8,128)(2,1)} %bitcast.4, f32[3,3,256]{2,1,0:T(4,128)} %short.1, f32[128,256]{1,0:T(8,128)} %taps.1, f32[1,256]{1,0:T(1,128)} %bitcast.6, f32[1,256]{1,0:T(1,128)} %bitcast.7, ...), custom_call_target="tpu_custom_call" | custom-call | tf_op jit(solution)/shard_map/pallas_call | solution.py:588
  76.2 2.3 %copy.14 = bf16[128,4096]{1,0:T(8,128)(2,1)} copy(bf16[128,4096]{1,0:T(8,128)(2,1)} %shard_map.118) | data formatting | bytes 2097152

commit v3 on v2

--- a/solution.py
+++ b/solution.py
@@ -528,13 +528,13 @@
     keep(0)
     start(gated_mine(0))
     relay((6,))
+    w_ready(2)
+    multiply(2, 1, 3)
+    send_own(2, early)
     gated_ready(0)
-    for r in range(2):
+    for r in range(3):
         multiply(r, 0, 1)
         send_own(r, late)
-    w_ready(2)
-    multiply(2, 0, 4)
-    send_own(2, None)
     relay((3, 7))
     for r in range(2):
         pass_on(r, early)

time: 78.7 us -> 76.1 us (0.967)
  Pallas kernels: 76.2 us -> 73.6 us
    pallas_call x1, Pallas kernels: 76.2 us -> 73.6 us  [shards(): pl.pallas_call(kernel, out_shape=jax.ShapeDtypeStruct((128, 4096), BF16),...]
where the time goes in v3:
time: 76.1 us; the launch traced here: 75.9 us
  Pallas kernels  73.6 us (97%)
  local copies, waits for them, and re-layouts  2.29 us (3%)
    pallas_call x1, Pallas kernels, shards(): pl.pallas_call(kernel, out_shape=jax.ShapeDtypeStruct((128, 4096), BF16),...  73.6 us
    unnamed x1, local copies, waits for them, and re-layouts  2.29 us

profile of v3, /device:TPU:1, one launch (start us, length us, event | category | flops | bytes accessed | tf_op | source)
XLA Modules:
  0.0 75.9 jit_solution(17769456585840297113)
XLA Ops:
  0.0 73.6 %shard_map.118 = bf16[128,4096]{1,0:T(8,128)(2,1)} custom-call(bf16[2048,4096]{1,0:T(8,128)(2,1)} %tokens.1, f32[1,4096]{1,0:T(1,128)} %bitcast.5, bf16[3,4096,256]{2,1,0:T(8,128)(2,1)} %bitcast.4, f32[3,3,256]{2,1,0:T(4,128)} %short.1, f32[128,256]{1,0:T(8,128)} %taps.1, f32[1,256]{1,0:T(1,128)} %bitcast.6, f32[1,256]{1,0:T(1,128)} %bitcast.7, ...), custom_call_target="tpu_custom_call" | custom-call | tf_op jit(solution)/shard_map/pallas_call | solution.py:588
  73.6 2.3 %copy.14 = bf16[128,4096]{1,0:T(8,128)(2,1)} copy(bf16[128,4096]{1,0:T(8,128)(2,1)} %shard_map.118) | data formatting | bytes 2097152

commit v4 on v3

--- a/solution.py
+++ b/solution.py
@@ -521,21 +521,23 @@
         multiply(r, 1, 3)
         send_own(r, early)
 
+    relay((6,))
     z_copy.wait_recv()
     filter_first(0)
     start(gated_other(0))
     filter_first(1)
     keep(0)
     start(gated_mine(0))
-    relay((6,))
     w_ready(2)
     multiply(2, 1, 3)
     send_own(2, early)
+    relay((7,))
     gated_ready(0)
     for r in range(3):
         multiply(r, 0, 1)
         send_own(r, late)
-    relay((3, 7))
+        if r == 1:
+            relay((3,))
     for r in range(2):
         pass_on(r, early)
     w_ready(3)

time: 76.1 us -> 76.2 us (level)
  no operation moved by 1% of the time
where the time goes in v4:
time: 76.2 us; the launch traced here: 76 us
  Pallas kernels  73.7 us (97%)
  local copies, waits for them, and re-layouts  2.29 us (3%)
    pallas_call x1, Pallas kernels, shards(): pl.pallas_call(kernel, out_shape=jax.ShapeDtypeStruct((128, 4096), BF16),...  73.7 us
    unnamed x1, local copies, waits for them, and re-layouts  2.29 us

profile of v4, /device:TPU:1, one launch (start us, length us, event | category | flops | bytes accessed | tf_op | source)
XLA Modules:
  0.0 76.0 jit_solution(2505429308752468736)
XLA Ops:
  0.0 73.7 %shard_map.118 = bf16[128,4096]{1,0:T(8,128)(2,1)} custom-call(bf16[2048,4096]{1,0:T(8,128)(2,1)} %tokens.1, f32[1,4096]{1,0:T(1,128)} %bitcast.5, bf16[3,4096,256]{2,1,0:T(8,128)(2,1)} %bitcast.4, f32[3,3,256]{2,1,0:T(4,128)} %short.1, f32[128,256]{1,0:T(8,128)} %taps.1, f32[1,256]{1,0:T(1,128)} %bitcast.6, f32[1,256]{1,0:T(1,128)} %bitcast.7, ...), custom_call_target="tpu_custom_call" | custom-call | tf_op jit(solution)/shard_map/pallas_call | solution.py:590
  73.7 2.3 %copy.14 = bf16[128,4096]{1,0:T(8,128)(2,1)} copy(bf16[128,4096]{1,0:T(8,128)(2,1)} %shard_map.118) | data formatting | bytes 2097152
